TPU v7x, 32 devices: a whole 2x2x4 slice. The times are simulated.
32 devices in a mesh: ctx: 8 (over z, x), fsdp: 4 (over y, core).
Axes of the slice: x: 2, y: 2, z: 4, core: 2. Of those that a mesh axis runs over, the one named last changes fastest.
Arguments:
- inputs: bfloat16 [4, 1024, 768], P('fsdp', 'ctx'), may hold values from -6 to 6
- block_order: int32 [16], replicated, may hold values from 0 to 15, each once
- cotangent: bfloat16 [4, 1024, 768], P('fsdp', 'ctx'), may hold values from -6 to 6
- first_gain: bfloat16 [768], P('fsdp'), may hold values from 0.25 to 1.75
- first_shift: bfloat16 [768], P('fsdp'), may hold values from -3 to 3
- qkv_weight: bfloat16 [768, 2304], P('fsdp')
- qv_bias: bfloat16 [1536], P('fsdp'), may hold values from -3 to 3
- proj_weight: bfloat16 [768, 768], P('fsdp'), may hold values from -1.75 to 1.75
- proj_bias: bfloat16 [768], P('fsdp'), may hold values from -3 to 3
- second_gain: bfloat16 [768], P('fsdp'), may hold values from 0.25 to 1.75
- second_shift: bfloat16 [768], P('fsdp'), may hold values from -3 to 3
- fc_weight: bfloat16 [768, 3072], P('fsdp'), may hold values from -0.21875 to 0.21875
- fc_bias: bfloat16 [3072], P('fsdp'), may hold values from -3 to 3
- down_weight: bfloat16 [3072, 768], P('fsdp'), may hold values from -0.109375 to 0.109375
- down_bias: bfloat16 [768], P('fsdp'), may hold values from -3 to 3
Outputs:
- block_out: bfloat16 [4, 1024, 768], P('fsdp', 'ctx')
- grad_input: float32 [4, 1024, 768], P('fsdp', 'ctx')
- grad_first_gain: float32 [768], P(('ctx', 'fsdp'))
- grad_first_shift: float32 [768], P(('ctx', 'fsdp'))
- grad_qkv_weight: float32 [768, 2304], P('fsdp', 'ctx')
- grad_qv_bias: float32 [1536], P(('ctx', 'fsdp'))
- grad_proj_weight: float32 [768, 768], P('fsdp', 'ctx')
- grad_proj_bias: float32 [768], P(('ctx', 'fsdp'))
- grad_second_gain: float32 [768], P(('ctx', 'fsdp'))
- grad_second_shift: float32 [768], P(('ctx', 'fsdp'))
- grad_fc_weight: float32 [768, 3072], P('fsdp', 'ctx')
- grad_fc_bias: float32 [3072], P(('ctx', 'fsdp'))
- grad_down_weight: float32 [3072, 768], P('fsdp', 'ctx')
- grad_down_bias: float32 [768], P(('ctx', 'fsdp'))
Inputs may be any that keep to these rules, and one draw needn't show every extreme that they name: `block_order`: a permutation of 0 to 15.
All inputs are finite; a program needn't handle non-finite values.
Results may differ from a plain program's by a relative error of at most 0.033.
Values may be sent and summed in bfloat16 or wider, within the bound.
No kernel may reach another device: no remote copies, remote signals or barrier semaphores. Data moves between devices by JAX's collectives and lax.ppermute only.
A program may use at most 256 MiB of HBM per device.

v0:
```python
import math
import jax
import jax.numpy as jnp
from jax import lax
from jax.sharding import PartitionSpec as P

H = 12
HD = 64
epsilon = 1e-05
negative_big = -1e30
gelu_coeff = 0.7978845608028654


def from_behind(value, axis, steps):
    count = lax.axis_size(axis)
    pairs = [(source, (source + steps) % count) for source in range(count)]
    return lax.ppermute(value, axis, pairs)


def split_heads(matrix):
    return matrix.reshape(matrix.shape[0], H, HD)


def norm_forward(rows_in, norm_gain, norm_shift):
    center = rows_in - jnp.mean(rows_in, axis=-1, keepdims=True)
    inverse = lax.rsqrt(jnp.mean(center * center, axis=-1, keepdims=True) + epsilon)
    normed = center * inverse
    return (normed, inverse, (normed * norm_gain + norm_shift).astype(jnp.bfloat16))


def norm_backward(grad_out, normed, inverse, norm_gain):
    scaled = grad_out * norm_gain
    return inverse * (
        scaled
        - jnp.mean(scaled, axis=-1, keepdims=True)
        - normed * jnp.mean(scaled * normed, axis=-1, keepdims=True)
    )


def gelu_pair(hidden_pre):
    argument = gelu_coeff * (hidden_pre + 0.044715 * hidden_pre * hidden_pre * hidden_pre)
    tangent = jnp.tanh(argument)
    result = 0.5 * hidden_pre * (1.0 + tangent)
    derivative = 0.5 * (1.0 + tangent) + 0.5 * hidden_pre * (
        1.0 - tangent * tangent
    ) * gelu_coeff * (1.0 + 3.0 * 0.044715 * hidden_pre * hidden_pre)
    return (result, derivative)


def times_transposed(left_side, right_side):
    return lax.dot_general(
        left_side, right_side, (((1,), (1,)), ((), ())), preferred_element_type=jnp.float32
    )


def transposed_times(left_side, right_side):
    return lax.dot_general(
        left_side, right_side, (((0,), (0,)), ((), ())), preferred_element_type=jnp.float32
    )


def positions_of(block_order, first_row, row_count, block_rows):
    row_ids = first_row + jnp.arange(row_count, dtype=jnp.int32)
    owners = row_ids // block_rows
    matches = owners[:, None] == jnp.arange(block_order.shape[0], dtype=jnp.int32)[None, :]
    blocks = jnp.sum(jnp.where(matches, block_order[None, :], 0), axis=1)
    return blocks * block_rows + row_ids % block_rows


def head_scores(queries, key_rows):
    return jnp.einsum(
        "qhd,khd->hqk",
        split_heads(queries),
        split_heads(key_rows),
        preferred_element_type=jnp.float32,
    ) * (1.0 / math.sqrt(HD))


def attend_block(carry, queries, key_rows, values, visible):

    def attend_compute(running):
        run_max, run_sum, accumulated = running
        scores = jnp.where(visible[None], head_scores(queries, key_rows), negative_big)
        new_max = jnp.maximum(run_max, jnp.max(scores, axis=2))
        weights = jnp.where(visible[None], jnp.exp(scores - new_max[:, :, None]), 0.0)
        factor = jnp.exp(run_max - new_max)
        mixed = jnp.einsum(
            "hqk,khd->qhd",
            weights.astype(jnp.bfloat16),
            split_heads(values),
            preferred_element_type=jnp.float32,
        )
        return (new_max, jnp.sum(weights, axis=2), accumulated * factor.T[:, :, None] + mixed)

    return lax.cond(jnp.any(visible), attend_compute, lambda running: running, carry)


def softmax_grads(queries, key_rows, values, attended_grad, lse_rows, delta_rows, visible):
    probs = jnp.where(
        visible[None], jnp.exp(head_scores(queries, key_rows) - lse_rows.T[:, :, None]), 0.0
    )
    prob_grad = jnp.einsum(
        "qhd,khd->hqk",
        split_heads(attended_grad),
        split_heads(values),
        preferred_element_type=jnp.float32,
    )
    score_grad = (probs * (prob_grad - delta_rows.T[:, :, None])).astype(jnp.bfloat16)
    return (probs, score_grad)


def both_block(carry, queries, key_rows, values, attended_grad, lse_rows, delta_rows, visible):

    def both_compute(totals):
        probs, score_grad = softmax_grads(
            queries, key_rows, values, attended_grad, lse_rows, delta_rows, visible
        )
        scale_factor = 1.0 / math.sqrt(HD)
        query_total = (
            totals[0]
            + jnp.einsum(
                "hqk,khd->qhd",
                score_grad,
                split_heads(key_rows),
                preferred_element_type=jnp.float32,
            )
            * scale_factor
        )
        key_total = (
            totals[1]
            + jnp.einsum(
                "hqk,qhd->khd", score_grad, split_heads(queries), preferred_element_type=jnp.float32
            )
            * scale_factor
        )
        value_total = totals[2] + jnp.einsum(
            "hqk,qhd->khd",
            probs.astype(jnp.bfloat16),
            split_heads(attended_grad),
            preferred_element_type=jnp.float32,
        )
        return (query_total, key_total, value_total)

    return lax.cond(jnp.any(visible), both_compute, lambda totals: totals, carry)


def on_device(
    inputs,
    block_order,
    cotangent,
    first_gain,
    first_shift,
    qkv_weight,
    qv_bias,
    proj_weight,
    proj_bias,
    second_gain,
    second_shift,
    fc_weight,
    fc_bias,
    down_weight,
    down_bias,
):
    (
        first_gain,
        first_shift,
        qkv_weight,
        qv_bias,
        proj_weight,
        proj_bias,
        second_gain,
        second_shift,
        fc_weight,
        fc_bias,
        down_weight,
        down_bias,
    ) = (
        lax.all_gather(first_gain, "fsdp", axis=0, tiled=True),
        lax.all_gather(first_shift, "fsdp", axis=0, tiled=True),
        lax.all_gather(qkv_weight, "fsdp", axis=0, tiled=True),
        lax.all_gather(qv_bias, "fsdp", axis=0, tiled=True),
        lax.all_gather(proj_weight, "fsdp", axis=0, tiled=True),
        lax.all_gather(proj_bias, "fsdp", axis=0, tiled=True),
        lax.all_gather(second_gain, "fsdp", axis=0, tiled=True),
        lax.all_gather(second_shift, "fsdp", axis=0, tiled=True),
        lax.all_gather(fc_weight, "fsdp", axis=0, tiled=True),
        lax.all_gather(fc_bias, "fsdp", axis=0, tiled=True),
        lax.all_gather(down_weight, "fsdp", axis=0, tiled=True),
        lax.all_gather(down_bias, "fsdp", axis=0, tiled=True),
    )
    tokens = inputs[0].astype(jnp.float32)
    upstream = cotangent[0]
    rows_dev = tokens.shape[0]
    block_rows = rows_dev // 2
    model_width = tokens.shape[1]
    block_slot = lax.axis_index("ctx")
    own_pos = positions_of(block_order, block_slot * rows_dev, rows_dev, block_rows)
    first_normed, first_inverse, first_hidden = norm_forward(tokens, first_gain, first_shift)
    projected = jnp.dot(first_hidden, qkv_weight, preferred_element_type=jnp.float32)
    queries = (projected[:, :model_width] + qv_bias[:model_width]).astype(jnp.bfloat16)
    key_rows = projected[:, model_width : 2 * model_width].astype(jnp.bfloat16)
    values = (projected[:, 2 * model_width :] + qv_bias[model_width:]).astype(jnp.bfloat16)
    start_state = (
        jnp.full((H, rows_dev), negative_big, jnp.float32),
        jnp.zeros((H, rows_dev), jnp.float32),
        jnp.zeros((rows_dev, H, HD), jnp.float32),
    )
    incoming = (
        lax.all_gather(key_rows, "ctx", axis=0, tiled=True),
        lax.all_gather(values, "ctx", axis=0, tiled=True),
    )
    key_pos = positions_of(block_order, jnp.int32(0), incoming[0].shape[0], block_rows)
    visible = key_pos[None, :] <= own_pos[:, None]
    run_max, run_sum, accumulated = attend_block(
        start_state, queries, incoming[0], incoming[1], visible
    )
    lse_rows = (run_max + jnp.log(run_sum)).T
    attended = (
        (accumulated / run_sum.T[:, :, None]).reshape(rows_dev, model_width).astype(jnp.bfloat16)
    )
    residual = (
        tokens + jnp.dot(attended, proj_weight, preferred_element_type=jnp.float32) + proj_bias
    )
    second_normed, second_inverse, second_hidden = norm_forward(residual, second_gain, second_shift)
    hidden_pre = jnp.dot(second_hidden, fc_weight, preferred_element_type=jnp.float32) + fc_bias
    activation, derivative = gelu_pair(hidden_pre)
    activation_b = activation.astype(jnp.bfloat16)
    block_out = (
        residual
        + jnp.dot(activation_b, down_weight, preferred_element_type=jnp.float32)
        + down_bias
    ).astype(jnp.bfloat16)
    upstream_f = upstream.astype(jnp.float32)
    down_wgrad = transposed_times(activation_b, upstream)
    down_bgrad = jnp.sum(upstream_f, axis=0)
    pre_grad = times_transposed(upstream, down_weight) * derivative
    pre_grad_b = pre_grad.astype(jnp.bfloat16)
    fc_wgrad = transposed_times(second_hidden, pre_grad_b)
    fc_bgrad = jnp.sum(pre_grad, axis=0)
    second_grad = times_transposed(pre_grad_b, fc_weight)
    second_ggrad = jnp.sum(second_grad * second_normed, axis=0)
    second_sgrad = jnp.sum(second_grad, axis=0)
    residual_grad = upstream_f + norm_backward(
        second_grad, second_normed, second_inverse, second_gain
    )
    residual_grad_b = residual_grad.astype(jnp.bfloat16)
    proj_wgrad = transposed_times(attended, residual_grad_b)
    proj_bgrad = jnp.sum(residual_grad, axis=0)
    attended_grad = times_transposed(residual_grad_b, proj_weight).astype(jnp.bfloat16)
    delta_rows = jnp.einsum(
        "qhd,qhd->qh",
        split_heads(attended_grad),
        split_heads(attended),
        preferred_element_type=jnp.float32,
    )
    zero_heads = jnp.zeros((rows_dev, H, HD), jnp.float32)
    cycle_count = lax.axis_size("ctx")

    def cycle_step(step_index, state):
        held_keys, held_values, query_total, key_total, value_total = state
        anchor = (block_slot - step_index) % cycle_count
        key_pos = positions_of(block_order, anchor * rows_dev, rows_dev, block_rows)
        visible = key_pos[None, :] <= own_pos[:, None]
        query_total, key_total, value_total = both_block(
            (query_total, key_total, value_total),
            queries,
            held_keys,
            held_values,
            attended_grad,
            lse_rows,
            delta_rows,
            visible,
        )
        held_keys, held_values, key_total, value_total = (
            from_behind(held_keys, "ctx", 1),
            from_behind(held_values, "ctx", 1),
            from_behind(key_total.astype(jnp.bfloat16), "ctx", 1).astype(key_total.dtype),
            from_behind(value_total.astype(jnp.bfloat16), "ctx", 1).astype(value_total.dtype),
        )
        return (held_keys, held_values, query_total, key_total, value_total)

    start_cycle = (key_rows, values, zero_heads, zero_heads, zero_heads)
    unused_keys, unused_values, query_grad, key_grad, value_grad = lax.fori_loop(
        0, cycle_count, cycle_step, start_cycle
    )
    query_grad = query_grad.reshape(rows_dev, model_width)
    key_grad = key_grad.reshape(rows_dev, model_width)
    value_grad = value_grad.reshape(rows_dev, model_width)
    qkv_grad = jnp.concatenate([query_grad, key_grad, value_grad], axis=1).astype(jnp.bfloat16)
    qkv_wgrad = transposed_times(first_hidden, qkv_grad)
    qv_bgrad = jnp.concatenate([jnp.sum(query_grad, axis=0), jnp.sum(value_grad, axis=0)])
    first_grad = times_transposed(qkv_grad, qkv_weight)
    first_ggrad = jnp.sum(first_grad * first_normed, axis=0)
    first_sgrad = jnp.sum(first_grad, axis=0)
    input_grad = residual_grad + norm_backward(first_grad, first_normed, first_inverse, first_gain)
    vector_terms = (
        first_ggrad,
        first_sgrad,
        qv_bgrad,
        proj_bgrad,
        second_ggrad,
        second_sgrad,
        fc_bgrad,
        down_bgrad,
    )
    vector_sums = (
        lax.psum_scatter(vector_terms[0], ("ctx", "fsdp"), scatter_dimension=0, tiled=True),
        lax.psum_scatter(vector_terms[1], ("ctx", "fsdp"), scatter_dimension=0, tiled=True),
        lax.psum_scatter(vector_terms[2], ("ctx", "fsdp"), scatter_dimension=0, tiled=True),
        lax.psum_scatter(vector_terms[3], ("ctx", "fsdp"), scatter_dimension=0, tiled=True),
        lax.psum_scatter(vector_terms[4], ("ctx", "fsdp"), scatter_dimension=0, tiled=True),
        lax.psum_scatter(vector_terms[5], ("ctx", "fsdp"), scatter_dimension=0, tiled=True),
        lax.psum_scatter(vector_terms[6], ("ctx", "fsdp"), scatter_dimension=0, tiled=True),
        lax.psum_scatter(vector_terms[7], ("ctx", "fsdp"), scatter_dimension=0, tiled=True),
    )
    matrix_terms = (qkv_wgrad, proj_wgrad, fc_wgrad, down_wgrad)
    row_sums = (
        lax.psum_scatter(
            matrix_terms[0].astype(jnp.bfloat16), "fsdp", scatter_dimension=0, tiled=True
        ).astype(jnp.float32),
        lax.psum_scatter(
            matrix_terms[1].astype(jnp.bfloat16), "fsdp", scatter_dimension=0, tiled=True
        ).astype(jnp.float32),
        lax.psum_scatter(
            matrix_terms[2].astype(jnp.bfloat16), "fsdp", scatter_dimension=0, tiled=True
        ).astype(jnp.float32),
        lax.psum_scatter(
            matrix_terms[3].astype(jnp.bfloat16), "fsdp", scatter_dimension=0, tiled=True
        ).astype(jnp.float32),
    )
    matrix_sums = (
        lax.psum_scatter(row_sums[0], "ctx", scatter_dimension=1, tiled=True),
        lax.psum_scatter(row_sums[1], "ctx", scatter_dimension=1, tiled=True),
        lax.psum_scatter(row_sums[2], "ctx", scatter_dimension=1, tiled=True),
        lax.psum_scatter(row_sums[3], "ctx", scatter_dimension=1, tiled=True),
    )
    return (
        block_out[None],
        input_grad[None],
        vector_sums[0],
        vector_sums[1],
        matrix_sums[0],
        vector_sums[2],
        matrix_sums[1],
        vector_sums[3],
        vector_sums[4],
        vector_sums[5],
        matrix_sums[2],
        vector_sums[6],
        matrix_sums[3],
        vector_sums[7],
    )


def solution(mesh):
    placed = (
        P("fsdp", "ctx", None),
        P(),
        P("fsdp", "ctx", None),
        P("fsdp"),
        P("fsdp"),
        P("fsdp", None),
        P("fsdp"),
        P("fsdp", None),
        P("fsdp"),
        P("fsdp"),
        P("fsdp"),
        P("fsdp", None),
        P("fsdp"),
        P("fsdp", None),
        P("fsdp"),
    )
    return jax.shard_map(
        on_device,
        mesh=mesh,
        in_specs=placed,
        out_specs=(
            P("fsdp", "ctx", None),
            P("fsdp", "ctx", None),
            P(("ctx", "fsdp")),
            P(("ctx", "fsdp")),
            P("fsdp", "ctx"),
            P(("ctx", "fsdp")),
            P("fsdp", "ctx"),
            P(("ctx", "fsdp")),
            P(("ctx", "fsdp")),
            P(("ctx", "fsdp")),
            P("fsdp", "ctx"),
            P(("ctx", "fsdp")),
            P("fsdp", "ctx"),
            P(("ctx", "fsdp")),
        ),
        check_vma=False,
    )
```

profile of v0, /device:TPU:0, one launch (start us, length us, event | category | flops | bytes accessed | tf_op | source)
XLA Modules:
  0.0 852.1 jit_solution(7596826350199663733)
XLA Ops:
  14.9 14.1 %all-reduce.15 = (bf16[768]{0:T(1024)(128)(2,1)S(1)}, bf16[768]{0:T(1024)(128)(2,1)S(1)}, bf16[768]{0:T(1024)(128)(2,1)S(1)}, bf16[768]{0:T(1024)(128)(2,1)S(1)}...) all-reduce(bf16[768]{0:T(1024)(128)(2,1)S(1)} %dynamic-update-slice, ...), channel_id=1, replica_groups=mesh['ctx'=8,'fsdp'=4] {'fsdp'}, use_global_device_ids=true, to_apply=%add.1 | all-reduce | flops 4608 | bytes 18432
  31.2 12.0 %all-gather.9.cloned.1.call-done = bf16[768,2304]{1,0:T(8,128)(2,1)} async-done(((bf16[192,2304]{1,0:T(8,128)(2,1)}), bf16[768,2304]{1,0:T(8,128)(2,1)}) %all-gather.9.cloned.1.call-update) | async-done | bytes 3538960 | tf_op jit(solution)/shard_map/all_gather | solution.py:180
  46.8 5.2 all-gather
  57.6 5.2 all-gather.1
  63.9 27.2 %all-gather.11.cloned.1.call-done = bf16[1024,768]{1,0:T(8,128)(2,1)} async-done(((bf16[128,768]{1,0:T(8,128)(2,1)}), bf16[1024,768]{1,0:T(8,128)(2,1)}) %all-gather.11.cloned.1.call-update) | async-done | bytes 1572880 | tf_op jit(solution)/shard_map/all_gather | solution.py:209
  91.1 45.3 %all-gather.13.cloned.1.call-done = bf16[1024,768]{1,0:T(8,128)(2,1)} async-done(((bf16[128,768]{1,0:T(8,128)(2,1)}), bf16[1024,768]{1,0:T(8,128)(2,1)}) %all-gather.13.cloned.1.call-update) | async-done | bytes 1572880 | tf_op jit(solution)/shard_map/all_gather | solution.py:210
  136.4 13.5 %conditional.2 = (f32[12,128]{1,0:T(8,128)S(1)}, f32[12,128]{1,0:T(8,128)S(1)}, f32[128,12,64]{0,2,1:T(8,128)S(1)}, f32[12,128]{1,0:T(8,128)S(1)}) conditional(s32[]{:T(128)} %convert_element_type.167, () %tuple.50, (pred[128,1024]{1,0:T(8,128)(4,1)}, bf16[128,768]{1,0:T(8,128)(2,1)S(1)}, bf16[1024,768]{1,0:T(8,128)(2,1)}, ...), branch_computations={%region_5.6_spmd, %region_6.9_spmd} | conditional | flops 423200256 | bytes 61829348 | solution.py:95
  144.6 5.1 fusion.9
  156.2 36.4 %all-gather.17.cloned.1.call-done = bf16[768,3072]{1,0:T(8,128)(2,1)} async-done(((bf16[192,3072]{1,0:T(8,128)(2,1)}), bf16[768,3072]{1,0:T(8,128)(2,1)}) %all-gather.17.cloned.1.call-update) | async-done | bytes 4718608 | tf_op jit(solution)/shard_map/all_gather | solution.py:186
  195.8 35.6 %all-gather.19.cloned.1.call-done = bf16[3072,768]{1,0:T(8,128)(2,1)} async-done(((bf16[768,768]{1,0:T(8,128)(2,1)}), bf16[3072,768]{1,0:T(8,128)(2,1)}) %all-gather.19.cloned.1.call-update) | async-done | bytes 4718608 | tf_op jit(solution)/shard_map/all_gather | solution.py:188
  231.5 5.0 fusion.85
  244.9 174.3 %while.25 = (s32[]{:T(128)}, bf16[128,768]{0,1:T(8,128)(2,1)S(1)}, bf16[128,768]{0,1:T(8,128)(2,1)S(1)}, f32[128,12,64]{0,2,1:T(8,128)S(1)}, f32[128,12,64]{0,2,...) while((s32[]{:T(128)}, bf16[128,768]{0,1:T(8,128)(2,1)S(1)}, ...), condition=%wide.region_18.19_spmd.clone, body=%wide.region_13.18_spmd.clone.sunk | while | flops 128329360 | bytes 15188138 | solution.py:283
  254.4 4.5 collective-permute-done.2
  258.9 4.2 collective-permute-done.3
  263.1 4.2 collective-permute-done
  276.7 6.3 collective-permute-done.2
  283.0 4.2 collective-permute-done.3
  287.2 4.2 collective-permute-done
  299.9 8.1 collective-permute-done.2
  321.2 9.2 %collective-permute-done.2 = bf16[128,12,64]{0,2,1:T(8,128)(2,1)S(1)} collective-permute-done((bf16[128,12,64]{0,2,1:T(8,128)(2,1)S(1)}, bf16[128,12,64]{0,2,1:T(8,128)(2,1)S(1)}, u32[]{:S(2)}, u32[]{:S(2)}) %collective-permute-start.2) | collective-permute-done | bytes 196640 | tf_op jit(solution)/shard_map/while/body/eval_jaxpr/ppermute | solution.py:17
  343.2 8.7 %collective-permute-done.2 = bf16[128,12,64]{0,2,1:T(8,128)(2,1)S(1)} collective-permute-done((bf16[128,12,64]{0,2,1:T(8,128)(2,1)S(1)}, bf16[128,12,64]{0,2,1:T(8,128)(2,1)S(1)}, u32[]{:S(2)}, u32[]{:S(2)}) %collective-permute-start.2) | collective-permute-done | bytes 196640 | tf_op jit(solution)/shard_map/while/body/eval_jaxpr/ppermute | solution.py:17
  365.2 7.5 collective-permute-done.2
  386.2 8.1 collective-permute-done.2
  406.4 6.5 collective-permute-done.2
  435.5 25.0 %reduce-scatter.15.cloned.1.call-done = bf16[192,2304]{1,0:T(8,128)(2,1)} async-done(((bf16[768,2304]{1,0:T(8,128)(2,1)}), bf16[192,2304]{1,0:T(8,128)(2,1)}) %reduce-scatter.15.cloned.1.call-update) | async-done | bytes 884752 | tf_op jit(solution)/shard_map/reduce_scatter | solution.py:318
  463.3 47.8 %reduce-scatter.19.cloned.1.call-done = bf16[192,3072]{1,0:T(8,128)(2,1)} async-done(((bf16[768,3072]{1,0:T(8,128)(2,1)}), bf16[192,3072]{1,0:T(8,128)(2,1)}) %reduce-scatter.19.cloned.1.call-update) | async-done | bytes 1179664 | tf_op jit(solution)/shard_map/reduce_scatter | solution.py:324
  514.1 47.4 %reduce-scatter.23.cloned.1.call-done = bf16[768,768]{1,0:T(8,128)(2,1)} async-done(((bf16[3072,768]{1,0:T(8,128)(2,1)}), bf16[768,768]{1,0:T(8,128)(2,1)}) %reduce-scatter.23.cloned.1.call-update) | async-done | bytes 1179664 | tf_op jit(solution)/shard_map/reduce_scatter | solution.py:327
  569.7 40.5 %all-reduce.14 = (f32[768]{0:T(1024)S(1)}, f32[768]{0:T(1024)S(1)}, f32[1536]{0:T(1024)S(1)}, f32[768]{0:T(1024)S(1)}, f32[768]{0:T(1024)S(1)}, /*index=5*/f32[7...) all-reduce(f32[768]{0:T(1024)} %get-tuple-element.608, ...), channel_id=2, replica_groups=mesh['ctx'=8,'fsdp'=4] {'ctx','fsdp'}, use_global_device_ids=true, to_apply=%region_22.23.clone | all-reduce | flops 9216 | bytes 73728
  621.7 6.4 reduce-scatter.27.cloned.1.call-done
  629.7 70.3 %reduce-scatter.25.cloned.1.call-done = f32[288,192]{1,0:T(8,128)} async-done(((f32[2304,192]{1,0:T(8,128)}), f32[288,192]{1,0:T(8,128)}) %reduce-scatter.25.cloned.1.call-update) | async-done | bytes 221200
  701.9 71.0 %reduce-scatter.21.cloned.1.call-done = f32[192,384]{1,0:T(8,128)} async-done(((f32[192,3072]{1,0:T(8,128)}), f32[192,384]{1,0:T(8,128)}) %reduce-scatter.21.cloned.1.call-update) | async-done | bytes 294928 | tf_op jit(solution)/shard_map/reduce_scatter | solution.py:334
  772.9 72.7 %reduce-scatter.29.cloned.1.call-done = f32[96,768]{1,0:T(8,128)} async-done(((f32[768,768]{1,0:T(8,128)}), f32[96,768]{1,0:T(8,128)}) %reduce-scatter.29.cloned.1.call-update) | async-done | bytes 294928
  (377 shorter events, 187.6 us)
Async XLA Ops:
  7.2 36.0 %all-gather.9.cloned.1.call-start = ((), (), s32[]{:S(2)}) async-start(), calls=%async_computation.8 | async-start | bytes 4423680 | tf_op jit(solution)/shard_map/all_gather | solution.py:180
  7.9 83.2 %all-gather.11.cloned.1.call-start = ((), (), s32[]{:S(2)}) async-start(), calls=%async_computation.9 | async-start | bytes 1769472 | tf_op jit(solution)/shard_map/all_gather | solution.py:209
  46.8 89.7 %all-gather.13.cloned.1.call-start = ((), (), s32[]{:S(2)}) async-start(), calls=%async_computation.10 | async-start | bytes 1769472 | tf_op jit(solution)/shard_map/all_gather | solution.py:210
  52.8 100.9 %all-gather.15.cloned.1.call-start = ((), (), s32[]{:S(2)}) async-start(), calls=%async_computation.11 | async-start | bytes 1474560 | tf_op jit(solution)/shard_map/all_gather | solution.py:182
  53.4 139.1 %all-gather.17.cloned.1.call-start = ((), (), s32[]{:S(2)}) async-start(), calls=%async_computation.12 | async-start | bytes 5898240 | tf_op jit(solution)/shard_map/all_gather | solution.py:186
  54.0 177.4 %all-gather.19.cloned.1.call-start = ((), (), s32[]{:S(2)}) async-start(), calls=%async_computation.13 | async-start | bytes 5898240 | tf_op jit(solution)/shard_map/all_gather | solution.py:188
  54.6 378.8 %reduce-scatter.17.cloned.1.call-start = ((), (), s32[]{:S(2)}) async-start(), calls=%async_computation.15 | async-start | bytes 1474560 | tf_op jit(solution)/shard_map/reduce_scatter | solution.py:321
  244.7 215.8 %reduce-scatter.15.cloned.1.call-start = ((), (), s32[]{:S(2)}) async-start(), calls=%async_computation.14 | async-start | bytes 4423680 | tf_op jit(solution)/shard_map/reduce_scatter | solution.py:318
  251.4 15.9 %collective-permute-start = (bf16[128,768]{0,1:T(8,128)(2,1)S(1)}, bf16[128,768]{0,1:T(8,128)(2,1)S(1)}, u32[]{:S(2)}, u32[]{:S(2)}) collective-permute-start(bf16[128,768]{0,1:T(8,128)(2,1)S(1)} %copy.103), channel_id=1, source_target_pairs={{0,4},{4,8},{8,12},{12,16},{16,20},{20,24},{24,28},{28,0},{1,5},{5... | collective-permute-start | bytes 589832 | tf_op jit(solution)/shard_map/while/body/eval_jaxpr/ppermute | solution.py:17
  252.9 17.9 %collective-permute-start.1 = (bf16[128,768]{0,1:T(8,128)(2,1)S(1)}, bf16[128,768]{0,1:T(8,128)(2,1)S(1)}, u32[]{:S(2)}, u32[]{:S(2)}) collective-permute-start(bf16[128,768]{0,1:T(8,128)(2,1)S(1)} %copy.104), channel_id=1, source_target_pairs={{0,4},{4,8},{8,12},{12,16},{16,20},{20,24},{24,28},{28,0},{1,5},{5... | collective-permute-start | bytes 589832 | tf_op jit(solution)/shard_map/while/body/eval_jaxpr/ppermute | solution.py:17
  275.5 15.9 %collective-permute-start = (bf16[128,768]{0,1:T(8,128)(2,1)S(1)}, bf16[128,768]{0,1:T(8,128)(2,1)S(1)}, u32[]{:S(2)}, u32[]{:S(2)}) collective-permute-start(bf16[128,768]{0,1:T(8,128)(2,1)S(1)} %copy.103), channel_id=1, source_target_pairs={{0,4},{4,8},{8,12},{12,16},{16,20},{20,24},{24,28},{28,0},{1,5},{5... | collective-permute-start | bytes 589832 | tf_op jit(solution)/shard_map/while/body/eval_jaxpr/ppermute | solution.py:17
  276.1 18.0 %collective-permute-start.1 = (bf16[128,768]{0,1:T(8,128)(2,1)S(1)}, bf16[128,768]{0,1:T(8,128)(2,1)S(1)}, u32[]{:S(2)}, u32[]{:S(2)}) collective-permute-start(bf16[128,768]{0,1:T(8,128)(2,1)S(1)} %copy.104), channel_id=1, source_target_pairs={{0,4},{4,8},{8,12},{12,16},{16,20},{20,24},{24,28},{28,0},{1,5},{5... | collective-permute-start | bytes 589832 | tf_op jit(solution)/shard_map/while/body/eval_jaxpr/ppermute | solution.py:17
  297.6 14.6 %collective-permute-start.3 = (bf16[128,12,64]{0,2,1:T(8,128)(2,1)S(1)}, bf16[128,12,64]{0,2,1:T(8,128)(2,1)S(1)}, u32[]{:S(2)}, u32[]{:S(2)}) collective-permute-start(bf16[128,12,64]{0,2,1:T(8,128)(2,1)S(1)} %convert_element_type.301), channel_id=1, source_target_pairs={{0,4},{4,8},{8,12},{12,16},{16,20},{20,24},{24,28},{28,0},{1,5},{5... | collective-permute-start | bytes 589832 | tf_op jit(solution)/shard_map/while/body/eval_jaxpr/ppermute | solution.py:17
  298.7 17.4 %collective-permute-start = (bf16[128,768]{0,1:T(8,128)(2,1)S(1)}, bf16[128,768]{0,1:T(8,128)(2,1)S(1)}, u32[]{:S(2)}, u32[]{:S(2)}) collective-permute-start(bf16[128,768]{0,1:T(8,128)(2,1)S(1)} %copy.103), channel_id=1, source_target_pairs={{0,4},{4,8},{8,12},{12,16},{16,20},{20,24},{24,28},{28,0},{1,5},{5... | collective-permute-start | bytes 589832 | tf_op jit(solution)/shard_map/while/body/eval_jaxpr/ppermute | solution.py:17
  298.8 19.4 %collective-permute-start.1 = (bf16[128,768]{0,1:T(8,128)(2,1)S(1)}, bf16[128,768]{0,1:T(8,128)(2,1)S(1)}, u32[]{:S(2)}, u32[]{:S(2)}) collective-permute-start(bf16[128,768]{0,1:T(8,128)(2,1)S(1)} %copy.104), channel_id=1, source_target_pairs={{0,4},{4,8},{8,12},{12,16},{16,20},{20,24},{24,28},{28,0},{1,5},{5... | collective-permute-start | bytes 589832 | tf_op jit(solution)/shard_map/while/body/eval_jaxpr/ppermute | solution.py:17
  320.0 14.6 %collective-permute-start.3 = (bf16[128,12,64]{0,2,1:T(8,128)(2,1)S(1)}, bf16[128,12,64]{0,2,1:T(8,128)(2,1)S(1)}, u32[]{:S(2)}, u32[]{:S(2)}) collective-permute-start(bf16[128,12,64]{0,2,1:T(8,128)(2,1)S(1)} %convert_element_type.301), channel_id=1, source_target_pairs={{0,4},{4,8},{8,12},{12,16},{16,20},{20,24},{24,28},{28,0},{1,5},{5... | collective-permute-start | bytes 589832 | tf_op jit(solution)/shard_map/while/body/eval_jaxpr/ppermute | solution.py:17
  321.1 16.6 %collective-permute-start = (bf16[128,768]{0,1:T(8,128)(2,1)S(1)}, bf16[128,768]{0,1:T(8,128)(2,1)S(1)}, u32[]{:S(2)}, u32[]{:S(2)}) collective-permute-start(bf16[128,768]{0,1:T(8,128)(2,1)S(1)} %copy.103), channel_id=1, source_target_pairs={{0,4},{4,8},{8,12},{12,16},{16,20},{20,24},{24,28},{28,0},{1,5},{5... | collective-permute-start | bytes 589832 | tf_op jit(solution)/shard_map/while/body/eval_jaxpr/ppermute | solution.py:17
  321.1 18.6 %collective-permute-start.1 = (bf16[128,768]{0,1:T(8,128)(2,1)S(1)}, bf16[128,768]{0,1:T(8,128)(2,1)S(1)}, u32[]{:S(2)}, u32[]{:S(2)}) collective-permute-start(bf16[128,768]{0,1:T(8,128)(2,1)S(1)} %copy.104), channel_id=1, source_target_pairs={{0,4},{4,8},{8,12},{12,16},{16,20},{20,24},{24,28},{28,0},{1,5},{5... | collective-permute-start | bytes 589832 | tf_op jit(solution)/shard_map/while/body/eval_jaxpr/ppermute | solution.py:17
  341.6 14.6 %collective-permute-start.3 = (bf16[128,12,64]{0,2,1:T(8,128)(2,1)S(1)}, bf16[128,12,64]{0,2,1:T(8,128)(2,1)S(1)}, u32[]{:S(2)}, u32[]{:S(2)}) collective-permute-start(bf16[128,12,64]{0,2,1:T(8,128)(2,1)S(1)} %convert_element_type.301), channel_id=1, source_target_pairs={{0,4},{4,8},{8,12},{12,16},{16,20},{20,24},{24,28},{28,0},{1,5},{5... | collective-permute-start | bytes 589832 | tf_op jit(solution)/shard_map/while/body/eval_jaxpr/ppermute | solution.py:17
  342.6 15.8 %collective-permute-start = (bf16[128,768]{0,1:T(8,128)(2,1)S(1)}, bf16[128,768]{0,1:T(8,128)(2,1)S(1)}, u32[]{:S(2)}, u32[]{:S(2)}) collective-permute-start(bf16[128,768]{0,1:T(8,128)(2,1)S(1)} %copy.103), channel_id=1, source_target_pairs={{0,4},{4,8},{8,12},{12,16},{16,20},{20,24},{24,28},{28,0},{1,5},{5... | collective-permute-start | bytes 589832 | tf_op jit(solution)/shard_map/while/body/eval_jaxpr/ppermute | solution.py:17
  342.6 17.8 %collective-permute-start.1 = (bf16[128,768]{0,1:T(8,128)(2,1)S(1)}, bf16[128,768]{0,1:T(8,128)(2,1)S(1)}, u32[]{:S(2)}, u32[]{:S(2)}) collective-permute-start(bf16[128,768]{0,1:T(8,128)(2,1)S(1)} %copy.104), channel_id=1, source_target_pairs={{0,4},{4,8},{8,12},{12,16},{16,20},{20,24},{24,28},{28,0},{1,5},{5... | collective-permute-start | bytes 589832 | tf_op jit(solution)/shard_map/while/body/eval_jaxpr/ppermute | solution.py:17
  363.2 15.0 %collective-permute-start = (bf16[128,768]{0,1:T(8,128)(2,1)S(1)}, bf16[128,768]{0,1:T(8,128)(2,1)S(1)}, u32[]{:S(2)}, u32[]{:S(2)}) collective-permute-start(bf16[128,768]{0,1:T(8,128)(2,1)S(1)} %copy.103), channel_id=1, source_target_pairs={{0,4},{4,8},{8,12},{12,16},{16,20},{20,24},{24,28},{28,0},{1,5},{5... | collective-permute-start | bytes 589832 | tf_op jit(solution)/shard_map/while/body/eval_jaxpr/ppermute | solution.py:17
  363.3 17.0 %collective-permute-start.1 = (bf16[128,768]{0,1:T(8,128)(2,1)S(1)}, bf16[128,768]{0,1:T(8,128)(2,1)S(1)}, u32[]{:S(2)}, u32[]{:S(2)}) collective-permute-start(bf16[128,768]{0,1:T(8,128)(2,1)S(1)} %copy.104), channel_id=1, source_target_pairs={{0,4},{4,8},{8,12},{12,16},{16,20},{20,24},{24,28},{28,0},{1,5},{5... | collective-permute-start | bytes 589832 | tf_op jit(solution)/shard_map/while/body/eval_jaxpr/ppermute | solution.py:17
  383.9 15.0 %collective-permute-start = (bf16[128,768]{0,1:T(8,128)(2,1)S(1)}, bf16[128,768]{0,1:T(8,128)(2,1)S(1)}, u32[]{:S(2)}, u32[]{:S(2)}) collective-permute-start(bf16[128,768]{0,1:T(8,128)(2,1)S(1)} %copy.103), channel_id=1, source_target_pairs={{0,4},{4,8},{8,12},{12,16},{16,20},{20,24},{24,28},{28,0},{1,5},{5... | collective-permute-start | bytes 589832 | tf_op jit(solution)/shard_map/while/body/eval_jaxpr/ppermute | solution.py:17
  384.0 17.1 %collective-permute-start.1 = (bf16[128,768]{0,1:T(8,128)(2,1)S(1)}, bf16[128,768]{0,1:T(8,128)(2,1)S(1)}, u32[]{:S(2)}, u32[]{:S(2)}) collective-permute-start(bf16[128,768]{0,1:T(8,128)(2,1)S(1)} %copy.104), channel_id=1, source_target_pairs={{0,4},{4,8},{8,12},{12,16},{16,20},{20,24},{24,28},{28,0},{1,5},{5... | collective-permute-start | bytes 589832 | tf_op jit(solution)/shard_map/while/body/eval_jaxpr/ppermute | solution.py:17
  403.2 16.0 %collective-permute-start.1 = (bf16[128,768]{0,1:T(8,128)(2,1)S(1)}, bf16[128,768]{0,1:T(8,128)(2,1)S(1)}, u32[]{:S(2)}, u32[]{:S(2)}) collective-permute-start(bf16[128,768]{0,1:T(8,128)(2,1)S(1)} %copy.104), channel_id=1, source_target_pairs={{0,4},{4,8},{8,12},{12,16},{16,20},{20,24},{24,28},{28,0},{1,5},{5... | collective-permute-start | bytes 589832 | tf_op jit(solution)/shard_map/while/body/eval_jaxpr/ppermute | solution.py:17
  422.9 88.2 %reduce-scatter.19.cloned.1.call-start = ((), (), s32[]{:S(2)}) async-start(), calls=%async_computation.16 | async-start | bytes 5898240 | tf_op jit(solution)/shard_map/reduce_scatter | solution.py:324
  427.6 133.8 %reduce-scatter.23.cloned.1.call-start = ((), (), s32[]{:S(2)}) async-start(), calls=%async_computation.18 | async-start | bytes 5898240 | tf_op jit(solution)/shard_map/reduce_scatter | solution.py:327
  433.3 194.8 %reduce-scatter.27.cloned.1.call-start = ((), (), s32[]{:S(2)}) async-start(), calls=%async_computation.20 | async-start | bytes 884736
  435.5 264.5 %reduce-scatter.25.cloned.1.call-start = ((), (), s32[]{:S(2)}) async-start(), calls=%async_computation.19 | async-start | bytes 2654208
  463.2 309.7 %reduce-scatter.21.cloned.1.call-start = ((), (), s32[]{:S(2)}) async-start(), calls=%async_computation.17 | async-start | bytes 2654208 | tf_op jit(solution)/shard_map/reduce_scatter | solution.py:334
  514.0 331.5 %reduce-scatter.29.cloned.1.call-start = ((), (), s32[]{:S(2)}) async-start(), calls=%async_computation.21 | async-start | bytes 2654208
  (59 other events, 515.7 us)
Sparse Core Ops, SparseCore 0:
  9.5 33.6 all-gather.8
  46.9 44.1 all-gather.10
  93.9 42.5 all-gather.12
  137.9 15.7 all-gather.14
  155.1 37.4 all-gather.16
  194.0 37.4 all-gather.18
  244.8 25.6 reduce-scatter.16
  423.0 37.4 reduce-scatter.14
  463.1 47.9 reduce-scatter.18
  513.4 47.9 reduce-scatter.22
  564.8 63.2 reduce-scatter.26
  631.4 68.5 reduce-scatter.24
  704.1 68.7 reduce-scatter.20
  776.8 68.7 reduce-scatter.28
where the time goes:
time: 853 us; the launch traced here: 852 us
  waiting for transfers between devices  632 us (74%)
  blocking collectives  65 us (8%)
  matrix products  48.1 us (6%)
  local copies, waits for them, and re-layouts  32.4 us (4%)
  other arithmetic  27.2 us (3%)
  starting transfers between devices  25.4 us (3%)
  between operations  15.7 us (2%)
    unnamed x17, waiting for transfers between devices  152 us
    ppermute x32, waiting for transfers between devices, from_behind(): return lax.ppermute(value, axis, pairs)  130 us
    reduce_scatter x1, waiting for transfers between devices, on_device(): lax.psum_scatter(row_sums[2], 'ctx', scatter_dimension=1, tiled=True)  71 us
    unnamed x2, blocking collectives  54.6 us
    reduce_scatter x1, waiting for transfers between devices, on_device(): lax.psum_scatter(matrix_terms[2].astype(jnp.bfloat16), 'fsdp', scatter_di...  47.8 us
    reduce_scatter x1, waiting for transfers between devices, on_device(): lax.psum_scatter(matrix_terms[3].astype(jnp.bfloat16), 'fsdp', scatter_di...  47.4 us
    all_gather x1, waiting for transfers between devices, on_device(): lax.all_gather(values, 'ctx', axis=0, tiled=True)  45.3 us
    all_gather x1, waiting for transfers between devices, on_device(): lax.all_gather(fc_weight, 'fsdp', axis=0, tiled=True)  36.4 us
  transfers between devices with their start and end apart: 46, of which 45 were waited for; matrix products, arithmetic and copies ran while one was open for 10% of the time, Pallas kernels for 0%

commit v1 on v0

--- a/solution.py
+++ b/solution.py
@@ -1,3 +1,4 @@
+import functools
 import math
 import jax
 import jax.numpy as jnp
@@ -9,6 +10,27 @@
 epsilon = 1e-05
 negative_big = -1e30
 gelu_coeff = 0.7978845608028654
+
+
+def convert_views(local_values, dim_k):
+    heard = lax.axis_size("ctx")
+    oldest = lax.axis_index("ctx")
+    low, value_now, plain = (heard, oldest, local_values.shape[dim_k])
+    all_rows = [b * low if no == dim_k else b for no, b in enumerate(local_values.shape)]
+    back = lax.dynamic_update_slice_in_dim(
+        jnp.zeros(all_rows, local_values.dtype), local_values, value_now * plain, axis=dim_k
+    )
+    for dev in range(1, low):
+        local_values = lax.ppermute(
+            local_values, "ctx", [(no, (no + 1) % low) for no in range(low)]
+        )
+        back = lax.dynamic_update_slice_in_dim(
+            back, local_values, (value_now - dev) % low * plain, axis=dim_k
+        )
+    return back
+
+
+extend_threads_by_axis = functools.partial(convert_views, dim_k=0)
 
 
 def from_behind(value, axis, steps):
@@ -205,10 +227,7 @@
         jnp.zeros((H, rows_dev), jnp.float32),
         jnp.zeros((rows_dev, H, HD), jnp.float32),
     )
-    incoming = (
-        lax.all_gather(key_rows, "ctx", axis=0, tiled=True),
-        lax.all_gather(values, "ctx", axis=0, tiled=True),
-    )
+    incoming = (lax.all_gather(key_rows, "ctx", axis=0, tiled=True), extend_threads_by_axis(values))
     key_pos = positions_of(block_order, jnp.int32(0), incoming[0].shape[0], block_rows)
     visible = key_pos[None, :] <= own_pos[:, None]
     run_max, run_sum, accumulated = attend_block(

time: 853 us -> 822 us (0.964)
  waiting for transfers between devices: 632 us -> 584 us
  local copies, waits for them, and re-layouts: 32.4 us -> 44.7 us
    ppermute x0 -> x7, waiting for transfers between devices: none -> 65.9 us  [convert_views(): lax.ppermute(local_values, 'ctx', [(no, (no + 1) % low) for no in range(l...]
    all_gather x1 -> x0, waiting for transfers between devices: 45.3 us -> none  [on_device(): lax.all_gather(values, 'ctx', axis=0, tiled=True)]
    all_gather x1, waiting for transfers between devices: 36.4 us -> 0.01 us  [on_device(): lax.all_gather(fc_weight, 'fsdp', axis=0, tiled=True)]
    all_gather x1, waiting for transfers between devices: 27.2 us -> 0.02 us  [on_device(): lax.all_gather(key_rows, 'ctx', axis=0, tiled=True)]
    unnamed x17 -> x16, waiting for transfers between devices: 152 us -> 152 us
    unnamed x108 -> x112, local copies, waits for them, and re-layouts: 27.7 us -> 27.4 us
  transfers between devices with their start and end apart: 46 -> 52, of which waited for: 45 -> 47; matrix products, arithmetic and copies ran while one was open for 10% -> 12% of each run, Pallas kernels for 0% -> 0%
where the time goes in v1:
time: 822 us; the launch traced here: 820 us
  waiting for transfers between devices  584 us (71%)
  blocking collectives  65.1 us (8%)
  matrix products  49 us (6%)
  local copies, waits for them, and re-layouts  44.7 us (5%)
  other arithmetic  28.6 us (3%)
  starting transfers between devices  26.9 us (3%)
  between operations  15.7 us (2%)
    unnamed x16, waiting for transfers between devices  152 us
    ppermute x32, waiting for transfers between devices, from_behind(): return lax.ppermute(value, axis, pairs)  130 us
    reduce_scatter x1, waiting for transfers between devices, on_device(): lax.psum_scatter(row_sums[2], 'ctx', scatter_dimension=1, tiled=True)  71 us
    ppermute x7, waiting for transfers between devices, convert_views(): lax.ppermute(local_values, 'ctx', [(no, (no + 1) % low) for no in range(l...  65.9 us
    unnamed x2, blocking collectives  54.7 us
    reduce_scatter x1, waiting for transfers between devices, on_device(): lax.psum_scatter(matrix_terms[2].astype(jnp.bfloat16), 'fsdp', scatter_di...  47.8 us
    reduce_scatter x1, waiting for transfers between devices, on_device(): lax.psum_scatter(matrix_terms[3].astype(jnp.bfloat16), 'fsdp', scatter_di...  47.5 us
    all_gather x1, waiting for transfers between devices, on_device(): lax.all_gather(down_weight, 'fsdp', axis=0, tiled=True)  32 us
  transfers between devices with their start and end apart: 52, of which 47 were waited for; matrix products, arithmetic and copies ran while one was open for 12% of the time, Pallas kernels for 0%

profile of v1, /device:TPU:0, one launch (start us, length us, event | category | flops | bytes accessed | tf_op | source)
XLA Modules:
  0.0 820.3 jit_solution(10244252191816707935)
XLA Ops:
  14.9 14.1 %all-reduce.15 = (bf16[768]{0:T(1024)(128)(2,1)S(1)}, bf16[768]{0:T(1024)(128)(2,1)S(1)}, bf16[768]{0:T(1024)(128)(2,1)S(1)}, bf16[768]{0:T(1024)(128)(2,1)S(1)}...) all-reduce(bf16[768]{0:T(1024)(128)(2,1)S(1)} %dynamic-update-slice, ...), channel_id=1, replica_groups=mesh['ctx'=8,'fsdp'=4] {'fsdp'}, use_global_device_ids=true, to_apply=%add.1 | all-reduce | flops 4608 | bytes 18432
  31.2 12.0 %all-gather.8.cloned.1.call-done = bf16[768,2304]{1,0:T(8,128)(2,1)} async-done(((bf16[192,2304]{1,0:T(8,128)(2,1)}), bf16[768,2304]{1,0:T(8,128)(2,1)}) %all-gather.8.cloned.1.call-update) | async-done | bytes 3538960 | tf_op jit(solution)/shard_map/all_gather | solution.py:202
  48.8 5.2 all-gather
  55.6 12.6 %collective-permute-done.4 = bf16[128,768]{1,0:T(8,128)(2,1)S(1)} collective-permute-done((bf16[128,768]{1,0:T(8,128)(2,1)S(1)}, bf16[128,768]{1,0:T(8,128)(2,1)S(1)}, u32[]{:S(2)}, u32[]{:S(2)}) %collective-permute-start.4) | collective-permute-done | bytes 196640 | tf_op jit(solution)/shard_map/ppermute | solution.py:24
  68.8 7.7 collective-permute-done.5
  76.7 13.1 %collective-permute-done.6 = bf16[128,768]{1,0:T(8,128)(2,1)S(1)} collective-permute-done((bf16[128,768]{1,0:T(8,128)(2,1)S(1)}, bf16[128,768]{1,0:T(8,128)(2,1)S(1)}, u32[]{:S(2)}, u32[]{:S(2)}) %collective-permute-start.6) | collective-permute-done | bytes 196640 | tf_op jit(solution)/shard_map/ppermute | solution.py:24
  89.9 12.9 %collective-permute-done.7 = bf16[128,768]{1,0:T(8,128)(2,1)S(1)} collective-permute-done((bf16[128,768]{1,0:T(8,128)(2,1)S(1)}, bf16[128,768]{1,0:T(8,128)(2,1)S(1)}, u32[]{:S(2)}, u32[]{:S(2)}) %collective-permute-start.7) | collective-permute-done | bytes 196640 | tf_op jit(solution)/shard_map/ppermute | solution.py:24
  102.8 10.2 %collective-permute-done.8 = bf16[128,768]{1,0:T(8,128)(2,1)S(1)} collective-permute-done((bf16[128,768]{1,0:T(8,128)(2,1)S(1)}, bf16[128,768]{1,0:T(8,128)(2,1)S(1)}, u32[]{:S(2)}, u32[]{:S(2)}) %collective-permute-start.8) | collective-permute-done | bytes 196640 | tf_op jit(solution)/shard_map/ppermute | solution.py:24
  113.0 9.3 %collective-permute-done.9 = bf16[128,768]{1,0:T(8,128)(2,1)S(1)} collective-permute-done((bf16[128,768]{1,0:T(8,128)(2,1)S(1)}, bf16[128,768]{1,0:T(8,128)(2,1)S(1)}, u32[]{:S(2)}, u32[]{:S(2)}) %collective-permute-start.9) | collective-permute-done | bytes 196640 | tf_op jit(solution)/shard_map/ppermute | solution.py:24
  124.5 5.2 all-gather.1
  130.9 27.9 %conditional.2 = (f32[12,128]{1,0:T(8,128)}, f32[12,128]{1,0:T(8,128)}, f32[128,12,64]{0,2,1:T(8,128)S(1)}, f32[12,128]{1,0:T(8,128)S(1)}) conditional(s32[]{:T(128)} %convert_element_type.170, () %tuple.121, (pred[128,1024]{1,0:T(8,128)(4,1)}, bf16[128,768]{1,0:T(8,128)(2,1)S(1)}, bf16[1024,768]{1,0:T(8,128)(2,1)}, s32[]{:T(128)}, ...), branch_computations={%region_5.6_spmd, %region_6.9_spmd.clone.clone} | conditional | flops 423200256 | bytes 69596552 | solution.py:117
  153.0 5.1 fusion.22
  165.9 32.0 %all-gather.16.cloned.1.call-done = bf16[3072,768]{1,0:T(8,128)(2,1)} async-done(((bf16[768,768]{1,0:T(8,128)(2,1)}), bf16[3072,768]{1,0:T(8,128)(2,1)}) %all-gather.16.cloned.1.call-update) | async-done | bytes 4718608 | tf_op jit(solution)/shard_map/all_gather | solution.py:210
  198.0 5.0 fusion.85
  212.0 174.2 %while.25 = (s32[]{:T(128)}, bf16[128,768]{0,1:T(8,128)(2,1)S(1)}, bf16[128,768]{0,1:T(8,128)(2,1)S(1)}, f32[128,12,64]{0,2,1:T(8,128)S(1)}, f32[128,12,64]{0,2,...) while((s32[]{:T(128)}, bf16[128,768]{0,1:T(8,128)(2,1)S(1)}, ...), condition=%wide.region_18.19_spmd.clone, body=%wide.region_13.18_spmd.clone.sunk | while | flops 128329360 | bytes 15188138 | solution.py:302
  221.5 4.5 collective-permute-done.2
  243.8 6.3 collective-permute-done.2
  250.1 4.2 collective-permute-done.3
  267.0 8.1 collective-permute-done.2
  288.3 9.2 %collective-permute-done.2 = bf16[128,12,64]{0,2,1:T(8,128)(2,1)S(1)} collective-permute-done((bf16[128,12,64]{0,2,1:T(8,128)(2,1)S(1)}, bf16[128,12,64]{0,2,1:T(8,128)(2,1)S(1)}, u32[]{:S(2)}, u32[]{:S(2)}) %collective-permute-start.2) | collective-permute-done | bytes 196640 | tf_op jit(solution)/shard_map/while/body/eval_jaxpr/ppermute | solution.py:39
  310.3 8.7 %collective-permute-done.2 = bf16[128,12,64]{0,2,1:T(8,128)(2,1)S(1)} collective-permute-done((bf16[128,12,64]{0,2,1:T(8,128)(2,1)S(1)}, bf16[128,12,64]{0,2,1:T(8,128)(2,1)S(1)}, u32[]{:S(2)}, u32[]{:S(2)}) %collective-permute-start.2) | collective-permute-done | bytes 196640 | tf_op jit(solution)/shard_map/while/body/eval_jaxpr/ppermute | solution.py:39
  332.2 7.5 collective-permute-done.2
  353.3 8.1 collective-permute-done.2
  373.5 6.4 collective-permute-done.2
  402.9 25.1 %reduce-scatter.15.cloned.1.call-done = bf16[192,2304]{1,0:T(8,128)(2,1)} async-done(((bf16[768,2304]{1,0:T(8,128)(2,1)}), bf16[192,2304]{1,0:T(8,128)(2,1)}) %reduce-scatter.15.cloned.1.call-update) | async-done | bytes 884752 | tf_op jit(solution)/shard_map/reduce_scatter | solution.py:337
  430.7 47.8 %reduce-scatter.19.cloned.1.call-done = bf16[192,3072]{1,0:T(8,128)(2,1)} async-done(((bf16[768,3072]{1,0:T(8,128)(2,1)}), bf16[192,3072]{1,0:T(8,128)(2,1)}) %reduce-scatter.19.cloned.1.call-update) | async-done | bytes 1179664 | tf_op jit(solution)/shard_map/reduce_scatter | solution.py:343
  481.5 47.5 %reduce-scatter.23.cloned.1.call-done = bf16[768,768]{1,0:T(8,128)(2,1)} async-done(((bf16[3072,768]{1,0:T(8,128)(2,1)}), bf16[768,768]{1,0:T(8,128)(2,1)}) %reduce-scatter.23.cloned.1.call-update) | async-done | bytes 1179664 | tf_op jit(solution)/shard_map/reduce_scatter | solution.py:346
  537.2 40.6 %all-reduce.14 = (f32[768]{0:T(1024)S(1)}, f32[768]{0:T(1024)S(1)}, f32[1536]{0:T(1024)S(1)}, f32[768]{0:T(1024)S(1)}, f32[768]{0:T(1024)S(1)}, /*index=5*/f32[7...) all-reduce(f32[768]{0:T(1024)} %get-tuple-element.1428, ...), channel_id=2, replica_groups=mesh['ctx'=8,'fsdp'=4] {'ctx','fsdp'}, use_global_device_ids=true, to_apply=%region_22.23.clone | all-reduce | flops 9216 | bytes 73728
  589.5 6.2 reduce-scatter.27.cloned.1.call-done
  597.4 70.7 %reduce-scatter.25.cloned.1.call-done = f32[288,192]{1,0:T(8,128)} async-done(((f32[2304,192]{1,0:T(8,128)}), f32[288,192]{1,0:T(8,128)}) %reduce-scatter.25.cloned.1.call-update) | async-done | bytes 221200
  669.8 71.0 %reduce-scatter.21.cloned.1.call-done = f32[192,384]{1,0:T(8,128)} async-done(((f32[192,3072]{1,0:T(8,128)}), f32[192,384]{1,0:T(8,128)}) %reduce-scatter.21.cloned.1.call-update) | async-done | bytes 294928 | tf_op jit(solution)/shard_map/reduce_scatter | solution.py:353
  740.8 73.0 %reduce-scatter.29.cloned.1.call-done = f32[96,768]{1,0:T(8,128)} async-done(((f32[768,768]{1,0:T(8,128)}), f32[96,768]{1,0:T(8,128)}) %reduce-scatter.29.cloned.1.call-update) | async-done | bytes 294928
  (408 shorter events, 214.1 us)
Async XLA Ops:
  7.2 36.0 %all-gather.8.cloned.1.call-start = ((), (), s32[]{:S(2)}) async-start(), calls=%async_computation.8 | async-start | bytes 4423680 | tf_op jit(solution)/shard_map/all_gather | solution.py:202
  7.9 122.9 %all-gather.10.cloned.1.call-start = ((), (), s32[]{:S(2)}) async-start(), calls=%async_computation.9 | async-start | bytes 1769472 | tf_op jit(solution)/shard_map/all_gather | solution.py:230
  46.8 113.4 %all-gather.12.cloned.1.call-start = ((), (), s32[]{:S(2)}) async-start(), calls=%async_computation.10 | async-start | bytes 1474560 | tf_op jit(solution)/shard_map/all_gather | solution.py:204
  47.5 115.1 %all-gather.14.cloned.1.call-start = ((), (), s32[]{:S(2)}) async-start(), calls=%async_computation.11 | async-start | bytes 5898240 | tf_op jit(solution)/shard_map/all_gather | solution.py:208
  48.1 149.8 %all-gather.16.cloned.1.call-start = ((), (), s32[]{:S(2)}) async-start(), calls=%async_computation.12 | async-start | bytes 5898240 | tf_op jit(solution)/shard_map/all_gather | solution.py:210
  48.7 352.0 %reduce-scatter.17.cloned.1.call-start = ((), (), s32[]{:S(2)}) async-start(), calls=%async_computation.14 | async-start | bytes 1474560 | tf_op jit(solution)/shard_map/reduce_scatter | solution.py:340
  211.2 216.7 %reduce-scatter.15.cloned.1.call-start = ((), (), s32[]{:S(2)}) async-start(), calls=%async_computation.13 | async-start | bytes 4423680 | tf_op jit(solution)/shard_map/reduce_scatter | solution.py:337
  218.6 15.9 %collective-permute-start = (bf16[128,768]{0,1:T(8,128)(2,1)S(1)}, bf16[128,768]{0,1:T(8,128)(2,1)S(1)}, u32[]{:S(2)}, u32[]{:S(2)}) collective-permute-start(bf16[128,768]{0,1:T(8,128)(2,1)S(1)} %copy.149), channel_id=1, source_target_pairs={{0,4},{4,8},{8,12},{12,16},{16,20},{20,24},{24,28},{28,0},{1,5},{5... | collective-permute-start | bytes 589832 | tf_op jit(solution)/shard_map/while/body/eval_jaxpr/ppermute | solution.py:39
  220.0 17.9 %collective-permute-start.1 = (bf16[128,768]{0,1:T(8,128)(2,1)S(1)}, bf16[128,768]{0,1:T(8,128)(2,1)S(1)}, u32[]{:S(2)}, u32[]{:S(2)}) collective-permute-start(bf16[128,768]{0,1:T(8,128)(2,1)S(1)} %copy.150), channel_id=1, source_target_pairs={{0,4},{4,8},{8,12},{12,16},{16,20},{20,24},{24,28},{28,0},{1,5},{5... | collective-permute-start | bytes 589832 | tf_op jit(solution)/shard_map/while/body/eval_jaxpr/ppermute | solution.py:39
  242.6 15.9 %collective-permute-start = (bf16[128,768]{0,1:T(8,128)(2,1)S(1)}, bf16[128,768]{0,1:T(8,128)(2,1)S(1)}, u32[]{:S(2)}, u32[]{:S(2)}) collective-permute-start(bf16[128,768]{0,1:T(8,128)(2,1)S(1)} %copy.149), channel_id=1, source_target_pairs={{0,4},{4,8},{8,12},{12,16},{16,20},{20,24},{24,28},{28,0},{1,5},{5... | collective-permute-start | bytes 589832 | tf_op jit(solution)/shard_map/while/body/eval_jaxpr/ppermute | solution.py:39
  243.2 18.0 %collective-permute-start.1 = (bf16[128,768]{0,1:T(8,128)(2,1)S(1)}, bf16[128,768]{0,1:T(8,128)(2,1)S(1)}, u32[]{:S(2)}, u32[]{:S(2)}) collective-permute-start(bf16[128,768]{0,1:T(8,128)(2,1)S(1)} %copy.150), channel_id=1, source_target_pairs={{0,4},{4,8},{8,12},{12,16},{16,20},{20,24},{24,28},{28,0},{1,5},{5... | collective-permute-start | bytes 589832 | tf_op jit(solution)/shard_map/while/body/eval_jaxpr/ppermute | solution.py:39
  264.7 14.6 %collective-permute-start.3 = (bf16[128,12,64]{0,2,1:T(8,128)(2,1)S(1)}, bf16[128,12,64]{0,2,1:T(8,128)(2,1)S(1)}, u32[]{:S(2)}, u32[]{:S(2)}) collective-permute-start(bf16[128,12,64]{0,2,1:T(8,128)(2,1)S(1)} %convert_element_type.306), channel_id=1, source_target_pairs={{0,4},{4,8},{8,12},{12,16},{16,20},{20,24},{24,28},{28,0},{1,5},{5... | collective-permute-start | bytes 589832 | tf_op jit(solution)/shard_map/while/body/eval_jaxpr/ppermute | solution.py:39
  265.8 17.4 %collective-permute-start = (bf16[128,768]{0,1:T(8,128)(2,1)S(1)}, bf16[128,768]{0,1:T(8,128)(2,1)S(1)}, u32[]{:S(2)}, u32[]{:S(2)}) collective-permute-start(bf16[128,768]{0,1:T(8,128)(2,1)S(1)} %copy.149), channel_id=1, source_target_pairs={{0,4},{4,8},{8,12},{12,16},{16,20},{20,24},{24,28},{28,0},{1,5},{5... | collective-permute-start | bytes 589832 | tf_op jit(solution)/shard_map/while/body/eval_jaxpr/ppermute | solution.py:39
  265.9 19.4 %collective-permute-start.1 = (bf16[128,768]{0,1:T(8,128)(2,1)S(1)}, bf16[128,768]{0,1:T(8,128)(2,1)S(1)}, u32[]{:S(2)}, u32[]{:S(2)}) collective-permute-start(bf16[128,768]{0,1:T(8,128)(2,1)S(1)} %copy.150), channel_id=1, source_target_pairs={{0,4},{4,8},{8,12},{12,16},{16,20},{20,24},{24,28},{28,0},{1,5},{5... | collective-permute-start | bytes 589832 | tf_op jit(solution)/shard_map/while/body/eval_jaxpr/ppermute | solution.py:39
  287.1 14.6 %collective-permute-start.3 = (bf16[128,12,64]{0,2,1:T(8,128)(2,1)S(1)}, bf16[128,12,64]{0,2,1:T(8,128)(2,1)S(1)}, u32[]{:S(2)}, u32[]{:S(2)}) collective-permute-start(bf16[128,12,64]{0,2,1:T(8,128)(2,1)S(1)} %convert_element_type.306), channel_id=1, source_target_pairs={{0,4},{4,8},{8,12},{12,16},{16,20},{20,24},{24,28},{28,0},{1,5},{5... | collective-permute-start | bytes 589832 | tf_op jit(solution)/shard_map/while/body/eval_jaxpr/ppermute | solution.py:39
  288.2 16.6 %collective-permute-start = (bf16[128,768]{0,1:T(8,128)(2,1)S(1)}, bf16[128,768]{0,1:T(8,128)(2,1)S(1)}, u32[]{:S(2)}, u32[]{:S(2)}) collective-permute-start(bf16[128,768]{0,1:T(8,128)(2,1)S(1)} %copy.149), channel_id=1, source_target_pairs={{0,4},{4,8},{8,12},{12,16},{16,20},{20,24},{24,28},{28,0},{1,5},{5... | collective-permute-start | bytes 589832 | tf_op jit(solution)/shard_map/while/body/eval_jaxpr/ppermute | solution.py:39
  288.2 18.6 %collective-permute-start.1 = (bf16[128,768]{0,1:T(8,128)(2,1)S(1)}, bf16[128,768]{0,1:T(8,128)(2,1)S(1)}, u32[]{:S(2)}, u32[]{:S(2)}) collective-permute-start(bf16[128,768]{0,1:T(8,128)(2,1)S(1)} %copy.150), channel_id=1, source_target_pairs={{0,4},{4,8},{8,12},{12,16},{16,20},{20,24},{24,28},{28,0},{1,5},{5... | collective-permute-start | bytes 589832 | tf_op jit(solution)/shard_map/while/body/eval_jaxpr/ppermute | solution.py:39
  308.6 14.6 %collective-permute-start.3 = (bf16[128,12,64]{0,2,1:T(8,128)(2,1)S(1)}, bf16[128,12,64]{0,2,1:T(8,128)(2,1)S(1)}, u32[]{:S(2)}, u32[]{:S(2)}) collective-permute-start(bf16[128,12,64]{0,2,1:T(8,128)(2,1)S(1)} %convert_element_type.306), channel_id=1, source_target_pairs={{0,4},{4,8},{8,12},{12,16},{16,20},{20,24},{24,28},{28,0},{1,5},{5... | collective-permute-start | bytes 589832 | tf_op jit(solution)/shard_map/while/body/eval_jaxpr/ppermute | solution.py:39
  309.7 15.8 %collective-permute-start = (bf16[128,768]{0,1:T(8,128)(2,1)S(1)}, bf16[128,768]{0,1:T(8,128)(2,1)S(1)}, u32[]{:S(2)}, u32[]{:S(2)}) collective-permute-start(bf16[128,768]{0,1:T(8,128)(2,1)S(1)} %copy.149), channel_id=1, source_target_pairs={{0,4},{4,8},{8,12},{12,16},{16,20},{20,24},{24,28},{28,0},{1,5},{5... | collective-permute-start | bytes 589832 | tf_op jit(solution)/shard_map/while/body/eval_jaxpr/ppermute | solution.py:39
  309.7 17.8 %collective-permute-start.1 = (bf16[128,768]{0,1:T(8,128)(2,1)S(1)}, bf16[128,768]{0,1:T(8,128)(2,1)S(1)}, u32[]{:S(2)}, u32[]{:S(2)}) collective-permute-start(bf16[128,768]{0,1:T(8,128)(2,1)S(1)} %copy.150), channel_id=1, source_target_pairs={{0,4},{4,8},{8,12},{12,16},{16,20},{20,24},{24,28},{28,0},{1,5},{5... | collective-permute-start | bytes 589832 | tf_op jit(solution)/shard_map/while/body/eval_jaxpr/ppermute | solution.py:39
  330.3 15.0 %collective-permute-start = (bf16[128,768]{0,1:T(8,128)(2,1)S(1)}, bf16[128,768]{0,1:T(8,128)(2,1)S(1)}, u32[]{:S(2)}, u32[]{:S(2)}) collective-permute-start(bf16[128,768]{0,1:T(8,128)(2,1)S(1)} %copy.149), channel_id=1, source_target_pairs={{0,4},{4,8},{8,12},{12,16},{16,20},{20,24},{24,28},{28,0},{1,5},{5... | collective-permute-start | bytes 589832 | tf_op jit(solution)/shard_map/while/body/eval_jaxpr/ppermute | solution.py:39
  330.4 17.0 %collective-permute-start.1 = (bf16[128,768]{0,1:T(8,128)(2,1)S(1)}, bf16[128,768]{0,1:T(8,128)(2,1)S(1)}, u32[]{:S(2)}, u32[]{:S(2)}) collective-permute-start(bf16[128,768]{0,1:T(8,128)(2,1)S(1)} %copy.150), channel_id=1, source_target_pairs={{0,4},{4,8},{8,12},{12,16},{16,20},{20,24},{24,28},{28,0},{1,5},{5... | collective-permute-start | bytes 589832 | tf_op jit(solution)/shard_map/while/body/eval_jaxpr/ppermute | solution.py:39
  351.0 15.0 %collective-permute-start = (bf16[128,768]{0,1:T(8,128)(2,1)S(1)}, bf16[128,768]{0,1:T(8,128)(2,1)S(1)}, u32[]{:S(2)}, u32[]{:S(2)}) collective-permute-start(bf16[128,768]{0,1:T(8,128)(2,1)S(1)} %copy.149), channel_id=1, source_target_pairs={{0,4},{4,8},{8,12},{12,16},{16,20},{20,24},{24,28},{28,0},{1,5},{5... | collective-permute-start | bytes 589832 | tf_op jit(solution)/shard_map/while/body/eval_jaxpr/ppermute | solution.py:39
  351.0 17.1 %collective-permute-start.1 = (bf16[128,768]{0,1:T(8,128)(2,1)S(1)}, bf16[128,768]{0,1:T(8,128)(2,1)S(1)}, u32[]{:S(2)}, u32[]{:S(2)}) collective-permute-start(bf16[128,768]{0,1:T(8,128)(2,1)S(1)} %copy.150), channel_id=1, source_target_pairs={{0,4},{4,8},{8,12},{12,16},{16,20},{20,24},{24,28},{28,0},{1,5},{5... | collective-permute-start | bytes 589832 | tf_op jit(solution)/shard_map/while/body/eval_jaxpr/ppermute | solution.py:39
  370.0 14.2 %collective-permute-start = (bf16[128,768]{0,1:T(8,128)(2,1)S(1)}, bf16[128,768]{0,1:T(8,128)(2,1)S(1)}, u32[]{:S(2)}, u32[]{:S(2)}) collective-permute-start(bf16[128,768]{0,1:T(8,128)(2,1)S(1)} %copy.149), channel_id=1, source_target_pairs={{0,4},{4,8},{8,12},{12,16},{16,20},{20,24},{24,28},{28,0},{1,5},{5... | collective-permute-start | bytes 589832 | tf_op jit(solution)/shard_map/while/body/eval_jaxpr/ppermute | solution.py:39
  370.3 16.0 %collective-permute-start.1 = (bf16[128,768]{0,1:T(8,128)(2,1)S(1)}, bf16[128,768]{0,1:T(8,128)(2,1)S(1)}, u32[]{:S(2)}, u32[]{:S(2)}) collective-permute-start(bf16[128,768]{0,1:T(8,128)(2,1)S(1)} %copy.150), channel_id=1, source_target_pairs={{0,4},{4,8},{8,12},{12,16},{16,20},{20,24},{24,28},{28,0},{1,5},{5... | collective-permute-start | bytes 589832 | tf_op jit(solution)/shard_map/while/body/eval_jaxpr/ppermute | solution.py:39
  390.3 88.2 %reduce-scatter.19.cloned.1.call-start = ((), (), s32[]{:S(2)}) async-start(), calls=%async_computation.15 | async-start | bytes 5898240 | tf_op jit(solution)/shard_map/reduce_scatter | solution.py:343
  395.0 134.0 %reduce-scatter.23.cloned.1.call-start = ((), (), s32[]{:S(2)}) async-start(), calls=%async_computation.17 | async-start | bytes 5898240 | tf_op jit(solution)/shard_map/reduce_scatter | solution.py:346
  400.7 195.0 %reduce-scatter.27.cloned.1.call-start = ((), (), s32[]{:S(2)}) async-start(), calls=%async_computation.19 | async-start | bytes 884736
  402.8 265.2 %reduce-scatter.25.cloned.1.call-start = ((), (), s32[]{:S(2)}) async-start(), calls=%async_computation.18 | async-start | bytes 2654208
  430.6 310.2 %reduce-scatter.21.cloned.1.call-start = ((), (), s32[]{:S(2)}) async-start(), calls=%async_computation.16 | async-start | bytes 2654208 | tf_op jit(solution)/shard_map/reduce_scatter | solution.py:353
  481.4 332.4 %reduce-scatter.29.cloned.1.call-start = ((), (), s32[]{:S(2)}) async-start(), calls=%async_computation.20 | async-start | bytes 2654208
  (67 other events, 836.6 us)
Sparse Core Ops, SparseCore 0:
  9.5 33.6 all-gather.7
  46.9 53.3 all-gather.9
  101.8 18.3 all-gather.11
  121.6 37.4 all-gather.13
  160.5 37.4 all-gather.15
  211.3 25.5 reduce-scatter.16
  390.4 37.4 reduce-scatter.14
  430.4 47.9 reduce-scatter.18
  481.0 47.9 reduce-scatter.22
  532.1 63.5 reduce-scatter.26
  599.2 68.7 reduce-scatter.24
  671.9 68.8 reduce-scatter.20
  744.9 68.8 reduce-scatter.28
